TPU v7x, 32 devices: a whole 2x2x4 slice. The times are simulated.
32 devices in a mesh: streams: 8 (over z, y), mp: 4 (over x, core).
Axes of the slice: x: 2, y: 2, z: 4, core: 2. Of those that a mesh axis runs over, the one named last changes fastest.
Arguments:
- frames: bfloat16 [3072, 1536], P('streams', 'mp'), may hold values from -6 to 6
- convolution_cache: bfloat16 [256, 31, 1536], P('streams', None, 'mp'), may hold values from -6 to 6
- destination: int32 [256], P('streams'), may hold values from 0 to 7, as said below
- tenant: int32 [256], P('streams'), may hold values from 0 to 3
- valid: int32 [256], P('streams'), may hold values from 1 to 4
- tenant_panel_slot: int32 [4], replicated, may hold values from 0 to 7, as said below
- input_weight: bfloat16 [1536, 2, 1536], P(None, None, 'mp'), may hold values from -0.15625 to 0.15625
- tenant_down_weight: bfloat16 [8, 1536, 16], P('streams', 'mp'), may hold values from -0.15625 to 0.15625
- tenant_up_weight: bfloat16 [8, 16, 2, 1536], P('streams', None, None, 'mp'), may hold values from -1.5 to 1.5
- depthwise_taps: float32 [32, 1536], P(None, 'mp'), may hold values from -1 to 1
- batchnorm_scale: float32 [1536], P('mp'), may hold values from 0.25 to 1.75
- batchnorm_offset: float32 [1536], P('mp'), may hold values from -3 to 3
Outputs:
- encoded: bfloat16 [3072, 1536], P('streams', 'mp')
Inputs may be any that keep to these rules, and one draw needn't show every extreme that they name: `destination`: for every slot index below 32, the streams in that slot of all devices go to distinct devices, so every device receives exactly one stream in each slot. One device sends exactly 4 streams to each device that it sends to. `tenant_panel_slot`: distinct slots.
All inputs are finite; a program needn't handle non-finite values.
Results may differ from a plain program's by a relative error of at most 0.0027.
Values may be sent and summed in bfloat16 or wider, within the bound.
A program may use at most 128 MiB of HBM per device.

v0:
```python
import jax
import jax.numpy as jnp
from jax import lax
from jax.sharding import PartitionSpec as P

CH = 3


def local(
    frames,
    convolution_cache,
    destination,
    tenant,
    valid,
    tenant_panel_slot,
    input_weight,
    tenant_down_weight,
    tenant_up_weight,
    depthwise_taps,
    batchnorm_scale,
    batchnorm_offset,
):
    peers = lax.axis_size("streams")
    stream_count = destination.shape[0]
    row_count, shard_width = frames.shape
    frame_count = row_count // stream_count
    cache_rows = convolution_cache.shape[1]
    per_peer = max(1, stream_count // peers)
    order = jnp.arange(stream_count, dtype=jnp.int32)
    same_target = destination[:, None] == destination[None, :]
    earlier = order[None, :] < order[:, None]
    rank = jnp.sum(jnp.where(same_target & earlier, 1, 0), axis=1).astype(jnp.int32)
    bucket = destination * per_peer + rank
    target = jnp.arange(peers * per_peer, dtype=jnp.int32)
    pick = bucket[None, :] == target[:, None]
    flat_cache = convolution_cache.reshape(stream_count, cache_rows * shard_width)
    outgoing = jnp.dot(
        pick.astype(jnp.bfloat16), flat_cache, preferred_element_type=jnp.float32
    ).astype(jnp.bfloat16)
    out_slot = jnp.sum(jnp.where(pick, order[None, :] + 1, 0), axis=1) - 1
    arrived, arrived_slot = (
        lax.all_to_all(
            outgoing.reshape(peers, per_peer, cache_rows * shard_width),
            "streams",
            split_axis=0,
            concat_axis=0,
            tiled=True,
        ),
        lax.all_to_all(
            out_slot.reshape(peers, per_peer), "streams", split_axis=0, concat_axis=0, tiled=True
        ),
    )
    place = arrived_slot.reshape(peers * per_peer)[None, :] == order[:, None]
    moved = jnp.dot(
        place.astype(jnp.bfloat16),
        arrived.reshape(peers * per_peer, cache_rows * shard_width),
        preferred_element_type=jnp.float32,
    ).astype(jnp.bfloat16)
    moved = moved.reshape(stream_count, cache_rows, shard_width)
    tenant_hit = tenant[:, None] == jnp.arange(tenant_panel_slot.shape[0], dtype=jnp.int32)[None, :]
    stream_slot = jnp.sum(jnp.where(tenant_hit, tenant_panel_slot[None, :], 0), axis=1)
    row_slot = jnp.repeat(stream_slot, frame_count)
    w_flat = input_weight.reshape(input_weight.shape[0], 2 * shard_width)
    whole = lax.all_gather(frames, "mp", axis=1, tiled=True)
    base = jnp.dot(whole, w_flat, preferred_element_type=jnp.float32)
    full_down = lax.all_gather(tenant_down_weight, "mp", axis=1, tiled=True)
    down_piece = lax.all_gather(full_down, "streams", axis=0, tiled=True)
    up_piece = lax.all_gather(tenant_up_weight, "streams", axis=0, tiled=True)
    hits = row_slot[:, None] == jnp.arange(down_piece.shape[0], dtype=jnp.int32)[None, :]
    projected = jnp.einsum("rd,pdk->rpk", whole, down_piece, preferred_element_type=jnp.float32)
    low_piece = jnp.sum(
        jnp.where(hits[:, :, None], projected, jnp.zeros_like(projected)), axis=1
    ).astype(jnp.bfloat16)
    count = up_piece.shape[0]
    spread = jnp.where(
        hits[:, :, None], low_piece[:, None, :], jnp.zeros_like(low_piece[:, None, :])
    ).reshape(row_count, count * low_piece.shape[1])
    lift = jnp.dot(
        spread,
        up_piece.reshape(count * low_piece.shape[1], 2 * shard_width),
        preferred_element_type=jnp.float32,
    )
    pre = base + lift
    gated = (pre[:, :shard_width] * jax.nn.sigmoid(pre[:, shard_width:])).astype(jnp.bfloat16)
    sequence = jnp.concatenate(
        [moved, gated.reshape(stream_count, frame_count, shard_width)], axis=1
    )

    def add_tap(tap_index, total):
        window = lax.dynamic_slice_in_dim(sequence, tap_index, frame_count, 1).astype(jnp.float32)
        weight = lax.dynamic_slice_in_dim(depthwise_taps, tap_index, 1, 0)
        return total + window * weight.reshape(1, 1, shard_width)

    mixed = lax.fori_loop(
        0,
        depthwise_taps.shape[0],
        add_tap,
        jnp.zeros((stream_count, frame_count, shard_width), jnp.float32),
    )
    normed = mixed * batchnorm_scale + batchnorm_offset
    active = normed * jax.nn.sigmoid(normed)
    frame_index = jnp.arange(frame_count, dtype=jnp.int32)
    keep = frame_index[None, :] < (valid * CH)[:, None]
    encoded = jnp.where(keep[:, :, None], active, jnp.zeros_like(active)).astype(jnp.bfloat16)
    return encoded.reshape(row_count, shard_width)


def solution(mesh):
    in_specs = (
        P("streams", "mp"),
        P("streams", None, "mp"),
        P("streams"),
        P("streams"),
        P("streams"),
        P(),
        P(None, None, "mp"),
        P("streams", "mp", None),
        P("streams", None, None, "mp"),
        P(None, "mp"),
        P("mp"),
        P("mp"),
    )
    out_specs = P("streams", "mp")
    return jax.shard_map(local, mesh=mesh, in_specs=in_specs, out_specs=out_specs, check_vma=False)
```

profile of v0, /device:TPU:0, one launch (start us, length us, event | category | flops | bytes accessed | tf_op | source)
XLA Modules:
  0.0 155.6 jit_solution(15587832560697222206)
XLA Ops:
  7.3 0.9 select_reduce_fusion.2
  9.6 7.3 %all-to-all-start = ((s32[8,1,4]{2,1,0:T(1,128)}), s32[8,1,4]{2,1,0:T(1,128)S(1)}, u32[]{:S(2)}, u32[]{:S(2)}) async-start(s32[8,1,4]{2,1,0:T(1,128)} %bitcast), calls=%async_computation | async-start | bytes 8192 | tf_op jit(solution)/shard_map/all_to_all | solution.py:49
  16.9 1.2 copy.25
  18.5 1.0 reshape.121
  19.5 3.8 %all-to-all-done = s32[8,1,4]{2,1,0:T(1,128)S(1)} async-done(((s32[8,1,4]{2,1,0:T(1,128)}), s32[8,1,4]{2,1,0:T(1,128)S(1)}, u32[]{:S(2)}, u32[]{:S(2)}) %all-to-all-start) | async-done | bytes 160 | tf_op jit(solution)/shard_map/all_to_all | solution.py:49
  23.3 3.5 %all-to-all-start.1 = ((bf16[8,4,11904]{2,1,0:T(4,128)(2,1)}), bf16[8,4,11904]{2,1,0:T(4,128)(2,1)S(1)}, u32[]{:S(2)}, u32[]{:S(2)}) async-start(bf16[8,4,11904]{2,1,0:T(4,128)(2,1)} %reshape.121), calls=%async_computation.1 | async-start | bytes 1523712 | tf_op jit(solution)/shard_map/all_to_all | solution.py:42
  26.9 3.6 %copy.26 = bf16[192,8,2,384]{3,1,2,0:T(8,128)(2,1)} copy(bf16[192,8,2,384]{3,2,1,0:T(2,128)(2,1)} %bitcast.22) | data formatting | bytes 4718592
  30.8 36.3 %all_gather.15 = bf16[8,16,2,384]{3,1,2,0:T(8,128)(2,1)S(1)} all-gather(bf16[1,16,2,384]{3,1,2,0:T(8,128)(2,1)S(1)} %copy.23), channel_id=1, replica_groups=mesh['streams'=8,'mp'=4] {'streams'}, dimensions={0}, use_global_device_ids=true | all-gather | bytes 221184 | tf_op jit(solution)/shard_map/all_gather | solution.py:68
  67.3 5.2 %all_gather.13 = bf16[1,1536,16]{1,2,0:T(8,128)(2,1)S(1)} all-gather(bf16[1,384,16]{1,2,0:T(8,128)(2,1)S(1)} %copy-done.2), channel_id=1, replica_groups=mesh['streams'=8,'mp'=4] {'mp'}, dimensions={1}, use_global_device_ids=true | all-gather | bytes 61440 | tf_op jit(solution)/shard_map/all_gather | solution.py:66
  72.5 31.2 %all_gather.14 = bf16[8,1536,16]{1,2,0:T(8,128)(2,1)S(1)} all-gather(bf16[1,1536,16]{1,2,0:T(8,128)(2,1)S(1)} %all_gather.13), channel_id=1, replica_groups=mesh['streams'=8,'mp'=4] {'streams'}, dimensions={0}, use_global_device_ids=true | all-gather | bytes 442368 | tf_op jit(solution)/shard_map/all_gather | solution.py:67
  106.2 1.9 %fusion.9 = f32[384,128]{0,1:S(1)} fusion(bf16[384,1536]{1,0:T(8,128)(2,1)} %all-gather.2.cloned.1.call-done, bf16[1536,128]{0,1:T(8,128)(2,1)S(1)} %bitcast.24), kind=kOutput, calls=%fused_computation.32 | convolution fusion | flops 150994944 | bytes 1769472
  108.1 2.7 %fusion.8 = f32[384,768]{1,0:T(8,128)S(1)} fusion(bf16[384,1536]{1,0:T(8,128)(2,1)S(1)} %copy-done, bf16[1536,768]{1,0:T(8,128)(2,1)} %bitcast.23), kind=kOutput, calls=%fused_computation.31 | convolution fusion | flops 905969664 | bytes 4718592 | tf_op jit(solution)/shard_map/dot_general | solution.py:65
  111.7 36.0 %while.14 = (s32[]{:T(128)}, f32[32,12,384]{2,1,0:T(8,128)S(1)}, bf16[32,43,384]{2,1,0:T(8,128)(2,1)S(1)}, f32[32,384]{1,0:T(8,128)}, s32[]{:T(128)}, /*index=5*/s32[]{:T(128)}) while((s32[]{:T(128)}, f32[32,12,384]{2,1,0:T(8,128)S(1)}, bf16[32,43,384]{2,1,0:T(8,128)(2,1)S(1)}, f32[32,384]{1,0:T(8,128)}, s32[]{:T(128)}, ...), condition=%wide.region_5.6_spmd.clone, body=%wide.region_4.5_spmd.clone.sunk | while | flops 589827 | bytes 1479263 | solution.py:94
  111.8 0.7 dynamic-slice_reduce_fusion.2
  112.9 0.7 dynamic-slice_reduce_fusion.2
  114.0 0.7 dynamic-slice_reduce_fusion.2
  115.1 0.7 dynamic-slice_reduce_fusion.2
  116.2 0.7 dynamic-slice_reduce_fusion.2
  117.4 0.7 dynamic-slice_reduce_fusion.2
  118.5 0.7 dynamic-slice_reduce_fusion.2
  119.6 0.7 dynamic-slice_reduce_fusion.2
  120.7 0.7 dynamic-slice_reduce_fusion.2
  121.8 0.7 dynamic-slice_reduce_fusion.2
  129.7 0.7 dynamic-slice_reduce_fusion.2
  130.8 0.7 dynamic-slice_reduce_fusion.2
  132.0 0.7 dynamic-slice_reduce_fusion.2
  133.1 0.7 dynamic-slice_reduce_fusion.2
  134.2 0.7 dynamic-slice_reduce_fusion.2
  135.4 0.7 dynamic-slice_reduce_fusion.2
  136.5 0.7 dynamic-slice_reduce_fusion.2
  137.6 0.7 dynamic-slice_reduce_fusion.2
  148.0 0.8 reshape.127
  (94 shorter events, 28.6 us)
Async XLA Ops:
  6.5 99.6 %all-gather.2.cloned.1.call-start = ((), (), s32[]{:S(2)}) async-start(), calls=%async_computation.2 | async-start | bytes 1474560 | tf_op jit(solution)/shard_map/all_gather | solution.py:64
  9.6 13.7 %all-to-all-start = ((s32[8,1,4]{2,1,0:T(1,128)}), s32[8,1,4]{2,1,0:T(1,128)S(1)}, u32[]{:S(2)}, u32[]{:S(2)}) async-start(s32[8,1,4]{2,1,0:T(1,128)} %bitcast), calls=%async_computation | async-start | bytes 8192 | tf_op jit(solution)/shard_map/all_to_all | solution.py:49
  23.3 81.8 %all-to-all-start.1 = ((bf16[8,4,11904]{2,1,0:T(4,128)(2,1)}), bf16[8,4,11904]{2,1,0:T(4,128)(2,1)S(1)}, u32[]{:S(2)}, u32[]{:S(2)}) async-start(bf16[8,4,11904]{2,1,0:T(4,128)(2,1)} %reshape.121), calls=%async_computation.1 | async-start | bytes 1523712 | tf_op jit(solution)/shard_map/all_to_all | solution.py:42
  26.9 3.6 %copy-start.5 = (s32[4]{0:T(128)S(1)}, s32[4]{0:T(128)}, u32[]{:S(2)}) copy-start(s32[4]{0:T(128)} %param.19) | copy-start | bytes 52
  26.9 3.6 %copy-start.6 = (s32[32]{0:T(128)S(1)}, s32[32]{0:T(128)}, u32[]{:S(2)}) copy-start(s32[32]{0:T(128)} %param.17) | copy-start | bytes 388
  26.9 3.9 %copy-start.1 = (bf16[1,16,2,384]{3,2,1,0:T(2,128)(2,1)S(1)}, bf16[1,16,2,384]{3,2,1,0:T(2,128)(2,1)}, u32[]{:S(2)}) copy-start(bf16[1,16,2,384]{3,2,1,0:T(2,128)(2,1)} %param.22) | copy-start | bytes 73732
  26.9 40.4 %copy-start.2 = (bf16[1,384,16]{1,2,0:T(8,128)(2,1)S(1)}, bf16[1,384,16]{1,2,0:T(8,128)(2,1)}, u32[]{:S(2)}) copy-start(bf16[1,384,16]{1,2,0:T(8,128)(2,1)} %param.21) | copy-start | bytes 36868
  30.5 73.3 %copy-start.7 = (s32[32]{0:T(128)S(1)}, s32[32]{0:T(128)}, u32[]{:S(2)}) copy-start(s32[32]{0:T(128)} %param.18) | copy-start | bytes 388
  106.2 2.0 %copy-start = (bf16[384,1536]{1,0:T(8,128)(2,1)S(1)}, bf16[384,1536]{1,0:T(8,128)(2,1)}, u32[]{:S(2)}) copy-start(bf16[384,1536]{1,0:T(8,128)(2,1)} %all-gather.2.cloned.1.call-done) | copy-start | bytes 3538948
  111.7 36.0 %copy-start.3 = (f32[384]{0:T(512)S(1)}, f32[384]{0:T(512)}, u32[]{:S(2)}) copy-start(f32[384]{0:T(512)} %param.25) | copy-start | bytes 4612
  111.7 36.0 %copy-start.4 = (f32[384]{0:T(512)S(1)}, f32[384]{0:T(512)}, u32[]{:S(2)}) copy-start(f32[384]{0:T(512)} %param.24) | copy-start | bytes 4612
Sparse Core Ops, SparseCore 0:
  8.9 20.1 all-gather.1
where the time goes:
time: 159 us; the launch traced here: 156 us
  blocking collectives  72.8 us (46%)
  local copies, waits for them, and re-layouts  32.5 us (20%)
  other arithmetic  15.2 us (10%)
  between operations  13.7 us (9%)
  starting transfers between devices  10.8 us (7%)
  matrix products  5.63 us (4%)
  waiting for transfers between devices  4.49 us (3%)
    all_gather x1, blocking collectives, local(): up_piece = lax.all_gather(tenant_up_weight, 'streams', axis=0, tiled=True)  36.3 us
    all_gather x1, blocking collectives, local(): down_piece = lax.all_gather(full_down, 'streams', axis=0, tiled=True)  31.2 us
    dynamic_slice x32, local copies, waits for them, and re-layouts, add_tap(): weight = lax.dynamic_slice_in_dim(depthwise_taps, tap_index, 1, 0)  23.4 us
    add x32, other arithmetic, add_tap(): return total + window * weight.reshape(1, 1, shard_width)  11.9 us
    all_to_all x1, starting transfers between devices, local(): lax.all_to_all(out_slot.reshape(peers, per_peer), 'streams', split_axis=0...  7.28 us
    all_gather x1, blocking collectives, local(): full_down = lax.all_gather(tenant_down_weight, 'mp', axis=1, tiled=True)  5.24 us
    all_to_all x1, waiting for transfers between devices, local(): lax.all_to_all(out_slot.reshape(peers, per_peer), 'streams', split_axis=0...  3.76 us
    unnamed x19, local copies, waits for them, and re-layouts  3.65 us
  transfers between devices with their start and end apart: 3, of which 1 were waited for; matrix products, arithmetic and copies ran while one was open for 7% of the time, Pallas kernels for 0%

commit v1 on v0

v1 whole, which is shorter than its diff:
```python
import functools

import jax
import jax.numpy as jnp
from jax import lax
from jax.experimental import pallas as pl
from jax.experimental.pallas import tpu as pltpu
from jax.sharding import PartitionSpec as P

CH = 3
MESH = pl.DeviceIdType.MESH
F32 = jnp.float32
BF16 = jnp.bfloat16


def iota(shape, dim):
    return lax.broadcasted_iota(jnp.int32, shape, dim)


def kernel(
    dims,
    pick_s, tenant_s, valid_s, panel_s,
    frames, cache, dest, weight_hbm, down, up, taps, scale, offset,
    out,
    gathered, outgoing, arrived, destall, downg, upg, lows, weight, acc, seq, enc,
    w_sem, f_send, f_recv, c_send, c_recv, d_send, d_recv, a_send, a_recv, u_send, u_recv,
    l_send, l_recv,
):
    peers, mps, count, fr, hist, width, per_peer, rank_dim = dims
    rows = count * fr
    me = lax.axis_index("streams")
    my = lax.axis_index("mp")

    w_copy = pltpu.make_async_copy(weight_hbm, weight, w_sem)
    w_copy.start()

    barrier = pltpu.get_barrier_semaphore()
    for o in range(1, mps):
        pl.semaphore_signal(
            barrier, inc=1, device_id={"mp": lax.rem(my + o, mps)}, device_id_type=MESH
        )

    def greet(o, c):
        pl.semaphore_signal(
            barrier, inc=1, device_id={"streams": lax.rem(me + o, peers)}, device_id_type=MESH
        )
        return c

    lax.fori_loop(1, peers, greet, 0)

    r_i, c_i = iota((rows, rows), 0), iota((rows, rows), 1)
    perm = jnp.where(c_i == (r_i % count) * fr + r_i // count, 1.0, 0.0).astype(BF16)
    mine = jnp.dot(perm, frames[...], preferred_element_type=F32).astype(BF16)
    gathered[my] = mine

    outgoing[:, hist:, :] = jnp.zeros((peers * per_peer, outgoing.shape[1] - hist, width), BF16)

    def pack(b, c):
        outgoing[b, :hist, :] = cache[pick_s[b]]
        return c

    lax.fori_loop(0, peers * per_peer, pack, 0)

    pl.semaphore_wait(barrier, peers - 1 + mps - 1)

    def remote(src, dst, send, recv, where):
        return pltpu.make_async_remote_copy(
            src_ref=src, dst_ref=dst, send_sem=send, recv_sem=recv,
            device_id=where, device_id_type=MESH,
        )

    def down_copy(o):
        to = {"streams": lax.rem(me + o, peers)}
        return remote(down, downg.at[me], a_send.at[o], a_recv.at[o], to)

    def up_copy(o):
        to = {"streams": lax.rem(me + o, peers)}
        return remote(up, upg.at[me], u_send.at[o], u_recv.at[o], to)

    def dest_copy(o):
        to = {"streams": lax.rem(me + o, peers)}
        return remote(dest, destall.at[me], d_send.at[o], d_recv.at[o], to)

    def cache_copy(o):
        to = lax.rem(me + o, peers)
        return remote(
            outgoing.at[pl.ds(to * per_peer, per_peer)],
            arrived.at[pl.ds(me * per_peer, per_peer)],
            c_send.at[o], c_recv.at[o], {"streams": to},
        )

    def frame_copy(o):
        to = {"mp": lax.rem(my + o, mps)}
        return remote(gathered.at[my], gathered.at[my], f_send.at[o], f_recv.at[o], to)

    def low_copy(o):
        to = {"mp": lax.rem(my + o, mps)}
        return remote(lows.at[my], lows.at[my], l_send.at[o], l_recv.at[o], to)

    def start_small(o, c):
        down_copy(o).start()
        return c

    def start_rest(o, c):
        up_copy(o).start()
        dest_copy(o).start()
        cache_copy(o).start()
        return c

    lax.fori_loop(1, peers, start_small, 0)
    for o in range(1, mps):
        frame_copy(o).start()
    lax.fori_loop(1, peers, start_rest, 0)

    downg[me] = down[...]
    upg[me] = up[...]
    destall[me] = dest[...]
    arrived[pl.ds(me * per_peer, per_peer)] = outgoing[pl.ds(me * per_peer, per_peer)]

    w_copy.wait()
    acc[...] = jnp.dot(
        mine, weight[pl.ds(pl.multiple_of(my * width, width), width), :],
        preferred_element_type=F32,
    )

    lane = iota((1, rows), 1) % count
    slot = jnp.zeros((1, rows), jnp.int32)
    for s in range(count):
        slot = jnp.where(lane == s, panel_s[tenant_s[s]], slot)

    def wait_down(o, c):
        down_copy(o).wait()
        return c

    lax.fori_loop(1, peers, wait_down, 0)
    panels = downg[...].reshape(peers * rank_dim, width)
    projected = lax.dot_general(
        panels, mine, (((1,), (1,)), ((), ())), preferred_element_type=F32
    )
    hit = iota((peers * rank_dim, rows), 0) // rank_dim == slot
    part = jnp.where(hit, projected, 0.0).reshape(peers, rank_dim, rows).sum(axis=0)
    lows[my] = part
    for o in range(1, mps):
        low_copy(o).start()

    def wait_small(o, c):
        dest_copy(o).wait()
        up_copy(o).wait()
        return c

    lax.fori_loop(1, peers, wait_small, 0)
    to_me = destall[:, 0, :] == me
    hits = jnp.where(to_me, 1.0, 0.0)
    tri = jnp.where(iota((128, 128), 0) < iota((128, 128), 1), 1.0, 0.0)
    earlier = jnp.dot(hits.astype(BF16), tri.astype(BF16), preferred_element_type=F32)
    owner = iota((peers, 128), 0).astype(F32)
    bucket = jnp.sum(hits * (owner * per_peer + earlier), axis=0, keepdims=True)
    eye = jnp.where(iota((128, 128), 0) == iota((128, 128), 1), 1.0, 0.0)
    column = lax.dot_general(
        eye.astype(BF16), jnp.broadcast_to(bucket, (128, 128)).astype(BF16),
        (((1,), (1,)), ((), ())), preferred_element_type=F32,
    )
    length = outgoing.shape[1]
    source = column[:count, :].astype(jnp.int32) * length

    for o in range(1, mps):
        low_copy(o).wait()
    low = lows[0]
    for j in range(1, mps):
        low = low + lows[j]
    low = low.astype(BF16).astype(F32)
    spread = jnp.where(
        hit, jnp.broadcast_to(low[None], (peers, rank_dim, rows)).reshape(peers * rank_dim, rows), 0.0
    )
    acc[...] += jnp.dot(
        spread.T.astype(BF16), upg[...].reshape(peers * rank_dim, 2 * width),
        preferred_element_type=F32,
    )

    for o in range(1, mps):
        frame_copy(o).wait()
        j = lax.rem(my + mps - o, mps)
        acc[...] += jnp.dot(
            gathered[j], weight[pl.ds(pl.multiple_of(j * width, width), width), :],
            preferred_element_type=F32,
        )
    pre = acc[...]
    gated = (pre[:, :width] * jax.nn.sigmoid(pre[:, width:])).astype(BF16)
    seq[pl.ds(hist, fr)] = gated.astype(F32).reshape(fr, count, width)

    def wait_cache(o, c):
        cache_copy(o).wait()
        return c

    lax.fori_loop(1, peers, wait_cache, 0)
    blocks = peers * per_peer * length
    flat = arrived[...].reshape(blocks, width)
    wanted = jnp.concatenate([source] * (blocks // 128), axis=1)
    wanted = wanted - iota((count, blocks), 1)
    select = jnp.concatenate(
        [jnp.where(wanted == -t, 1.0, 0.0).astype(BF16) for t in range(hist)], axis=0
    )
    moved = jnp.dot(select, flat, preferred_element_type=F32)
    seq[pl.ds(0, hist)] = moved.reshape(hist, count, width)

    limit = jnp.zeros((count, 128), jnp.int32)
    sub = iota((count, 128), 0)
    for s in range(count):
        limit = jnp.where(sub == s, valid_s[s] * CH, limit)
    seg = 8
    for sb in range(count // seg):
        keep = limit[sb * seg:(sb + 1) * seg][None] > iota((fr, seg, 128), 0)

        def column_block(cb, c, sb=sb, keep=keep):
            lanes = pl.ds(pl.multiple_of(cb * 128, 128), 128)
            total = jnp.zeros((fr, seg, 128), F32)
            for k in range(hist + 1):
                window = seq[pl.ds(k, fr), pl.ds(sb * seg, seg), lanes]
                total = total + window * taps[pl.ds(k, 1), lanes][None]
            normed = total * scale[:, lanes][None] + offset[:, lanes][None]
            active = normed * jax.nn.sigmoid(normed)
            enc[:, pl.ds(sb * seg, seg), lanes] = jnp.where(keep, active, 0.0)
            return c

        lax.fori_loop(0, width // 128, column_block, 0)
    back = jnp.where(r_i == (c_i % count) * fr + c_i // count, 1.0, 0.0).astype(BF16)
    out[...] = jnp.dot(
        back, enc[...].reshape(rows, width).astype(BF16), preferred_element_type=F32
    ).astype(BF16)


def local(
    frames, convolution_cache, destination, tenant, valid, tenant_panel_slot, input_weight,
    tenant_down_weight, tenant_up_weight, depthwise_taps, batchnorm_scale, batchnorm_offset,
):
    peers = lax.axis_size("streams")
    mps = lax.axis_size("mp")
    count = destination.shape[0]
    rows, width = frames.shape
    fr = rows // count
    hist = convolution_cache.shape[1]
    length = -(-hist // 16) * 16
    per_peer = max(1, count // peers)
    rank_dim = tenant_down_weight.shape[2]
    order = jnp.arange(count, dtype=jnp.int32)
    earlier = (destination[:, None] == destination[None, :]) & (order[None, :] < order[:, None])
    bucket = destination * per_peer + jnp.sum(earlier.astype(jnp.int32), axis=1)
    target = jnp.arange(peers * per_peer, dtype=jnp.int32)
    pick = jnp.sum(jnp.where(bucket[None, :] == target[:, None], order[None, :], 0), axis=1)
    dest = jnp.broadcast_to(
        jnp.pad(destination, (0, 128 - count), constant_values=-1)[None, :], (8, 128)
    )
    smem = pl.BlockSpec(memory_space=pltpu.SMEM)
    vmem = pl.BlockSpec(memory_space=pltpu.VMEM)
    dims = (peers, mps, count, fr, hist, width, per_peer, rank_dim)
    dma = pltpu.SemaphoreType.DMA
    return pl.pallas_call(
        functools.partial(kernel, dims),
        out_shape=jax.ShapeDtypeStruct((rows, width), BF16),
        in_specs=[smem] * 4 + [vmem] * 3 + [pl.BlockSpec(memory_space=pl.ANY)] + [vmem] * 5,
        out_specs=vmem,
        scratch_shapes=[
            pltpu.VMEM((mps, rows, width), BF16),
            pltpu.VMEM((peers * per_peer, length, width), BF16),
            pltpu.VMEM((peers * per_peer, length, width), BF16),
            pltpu.VMEM((peers, 8, 128), jnp.int32),
            pltpu.VMEM((peers, rank_dim, width), BF16),
            pltpu.VMEM((peers, rank_dim, 2 * width), BF16),
            pltpu.VMEM((mps, rank_dim, rows), F32),
            pltpu.VMEM((mps * width, 2 * width), BF16),
            pltpu.VMEM((rows, 2 * width), F32),
            pltpu.VMEM((hist + fr, count, width), F32),
            pltpu.VMEM((fr, count, width), F32),
            dma,
            dma((mps,)), dma((mps,)),
            dma((peers,)), dma((peers,)),
            dma((peers,)), dma((peers,)),
            dma((peers,)), dma((peers,)),
            dma((peers,)), dma((peers,)),
            dma((mps,)), dma((mps,)),
        ],
        compiler_params=pltpu.CompilerParams(
            collective_id=0, has_side_effects=True, vmem_limit_bytes=56 * 1024 * 1024
        ),
    )(
        pick, tenant, valid, tenant_panel_slot,
        frames, convolution_cache, dest,
        input_weight.reshape(mps * width, 2 * width),
        tenant_down_weight[0].T, tenant_up_weight.reshape(rank_dim, 2 * width),
        depthwise_taps, batchnorm_scale.reshape(1, width), batchnorm_offset.reshape(1, width),
    )


def solution(mesh):
    in_specs = (
        P("streams", "mp"),
        P("streams", None, "mp"),
        P("streams"),
        P("streams"),
        P("streams"),
        P(),
        P(None, None, "mp"),
        P("streams", "mp", None),
        P("streams", None, None, "mp"),
        P(None, "mp"),
        P("mp"),
        P("mp"),
    )
    return jax.shard_map(
        local, mesh=mesh, in_specs=in_specs, out_specs=P("streams", "mp"), check_vma=False
    )
```

time: 159 us -> 51 us (0.32)
  the two profiles are of different devices: /device:TPU:0 before, /device:TPU:28 now
where the time goes in v1:
time: 51 us; the launch traced here: 50.6 us
  Pallas kernels  35.6 us (70%)
  local copies, waits for them, and re-layouts  12.7 us (25%)
  other arithmetic  2.28 us (4%)
    pallas_call x1, Pallas kernels, local(): pl.pallas_call(functools.partial(kernel, dims), out_shape=jax.ShapeDtypeS...  35.6 us
    unnamed x4, local copies, waits for them, and re-layouts  8.88 us
    reshape x1, local copies, waits for them, and re-layouts, local(): batchnorm_offset.reshape(1, width)  1.27 us
    reshape x1, local copies, waits for them, and re-layouts, local(): batchnorm_scale.reshape(1, width)  1.26 us

profile of v1, /device:TPU:28, one launch (start us, length us, event | category | flops | bytes accessed | tf_op | source)
XLA Modules:
  0.0 50.6 jit_solution(10471583808229962877)
XLA Ops:
  0.0 0.7 %pad.4 = s32[128]{0:T(128)S(1)} pad(s32[32]{0:T(128)} %param.14, s32[]{:T(128)} %constant.2.clone.1), padding=0_96 | pad | bytes 644 | tf_op jit(solution)/shard_map/jit(_pad)/pad | solution.py:251
  0.7 0.9 %convert_reduce_fusion = s32[32]{0:T(128)S(1)} fusion(s32[32]{0:T(128)} %param.14), kind=kLoop, calls=%fused_computation.2 | loop fusion | flops 5088 | bytes 256 | tf_op jit(solution)/shard_map/reduce_sum | solution.py:247
  1.6 0.7 %multiply_add_fusion = s32[32]{0:T(128)S(1)} fusion(s32[32]{0:T(128)S(1)} %convert_reduce_fusion, s32[32]{0:T(128)} %param.14), kind=kLoop, calls=%fused_computation.5 | loop fusion | flops 64 | bytes 384 | tf_op jit(solution)/shard_map/add | solution.py:247
  2.2 0.7 %select_reduce_fusion.pick_s = s32[32]{0:T(128)} fusion(s32[32]{0:T(128)S(1)} %multiply_add_fusion), kind=kLoop, calls=%fused_computation | loop fusion | flops 3040 | bytes 256 | tf_op jit(solution)/shard_map/reduce_sum | solution.py:249
  2.9 1.3 %reshape.18.scale = f32[1,384]{1,0:T(1,128)} reshape(f32[384]{0:T(512)} %param.22) | data formatting | bytes 3072 | tf_op jit(solution)/shard_map/reshape | solution.py:290
  4.2 1.3 %reshape.19.offset = f32[1,384]{1,0:T(1,128)} reshape(f32[384]{0:T(512)} %param.23) | data formatting | bytes 3072 | tf_op jit(solution)/shard_map/reshape | solution.py:290
  5.5 0.6 %broadcast_in_dim.9.dest = s32[8,128]{1,0:T(8,128)} broadcast(s32[128]{0:T(128)S(1)} %pad.4), dimensions={1} | broadcast | bytes 4608 | tf_op jit(solution)/shard_map/broadcast_in_dim | solution.py:250
  6.1 1.3 %copy.16 = bf16[2,8,2,384]{3,1,2,0:T(8,128)(2,1)} copy(bf16[2,8,2,384]{3,2,1,0:T(2,128)(2,1)} %bitcast.11) | data formatting | bytes 49152
  7.4 2.3 %copy.14.cache = bf16[32,31,384]{2,1,0:T(8,128)(2,1)} copy(bf16[32,31,384]{2,0,1:T(8,128)(2,1)} %param.13) | data formatting | bytes 1523712 | tf_op args[1]
  9.7 3.5 %copy.15 = bf16[192,8,2,384]{3,1,2,0:T(8,128)(2,1)} copy(bf16[192,8,2,384]{3,2,1,0:T(2,128)(2,1)} %bitcast.9) | data formatting | bytes 4718592
  13.2 35.6 %shard_map.118 = bf16[384,384]{1,0:T(8,128)(2,1)} custom-call(s32[32]{0:T(128)} %select_reduce_fusion.pick_s, s32[32]{0:T(128)} %tenant_s.1, s32[32]{0:T(128)} %valid_s.1, s32[4]{0:T(128)} %panel_s.1, bf16[384,384]{1,0:T(8,128)(2,1)} %frames.1, bf16[32,31,384]{2,1,0:T(8,128)(2,1)} %copy.14.cache, s32[8,128]{1,0:T(8,128)} %broadcast_in_dim.9.dest, ...), custom_call_target="tpu_custom_call" | custom-call | tf_op jit(solution)/shard_map/pallas_call | solution.py:257
  48.9 1.7 %copy.18 = bf16[384,384]{1,0:T(8,128)(2,1)} copy(bf16[384,384]{1,0:T(8,128)(2,1)} %shard_map.118) | data formatting | bytes 589824

commit v2 on v1

--- a/solution.py
+++ b/solution.py
@@ -19,14 +19,14 @@
 
 def kernel(
     dims,
-    pick_s, tenant_s, valid_s, panel_s,
-    frames, cache, dest, weight_hbm, down, up, taps, scale, offset,
+    dest_s, tenant_s, valid_s, panel_s,
+    frames, cache, weight_hbm, down, up, taps, scale, offset,
     out,
-    gathered, outgoing, arrived, destall, downg, upg, lows, weight, acc, seq, enc,
+    gathered, outgoing, arrived, dest, destall, select, downg, upg, lows, weight, acc, seq, enc,
     w_sem, f_send, f_recv, c_send, c_recv, d_send, d_recv, a_send, a_recv, u_send, u_recv,
     l_send, l_recv,
 ):
-    peers, mps, count, fr, hist, width, per_peer, rank_dim = dims
+    peers, mps, count, fr, hist, length, width, per_peer, rank_dim = dims
     rows = count * fr
     me = lax.axis_index("streams")
     my = lax.axis_index("mp")
@@ -53,13 +53,20 @@
     mine = jnp.dot(perm, frames[...], preferred_element_type=F32).astype(BF16)
     gathered[my] = mine
 
-    outgoing[:, hist:, :] = jnp.zeros((peers * per_peer, outgoing.shape[1] - hist, width), BF16)
-
-    def pack(b, c):
-        outgoing[b, :hist, :] = cache[pick_s[b]]
-        return c
-
-    lax.fori_loop(0, peers * per_peer, pack, 0)
+    stream = iota((8, 128), 1) % count
+    goes = jnp.zeros((8, 128), jnp.int32)
+    for s in range(count):
+        goes = jnp.where(stream == s, dest_s[s], goes)
+    dest[...] = goes
+    place = jnp.zeros((8, 128), jnp.int32)
+    for s in range(count):
+        place = place + jnp.where((goes == dest_s[s]) & (stream > s), 1, 0)
+    chunk = length * per_peer
+    key = (goes * chunk + place)[:1]
+    lanes_all = hist * count
+    wide = -(-lanes_all // 128)
+    key = jnp.concatenate([key] * wide, axis=1)[:, :lanes_all]
+    key = key + (iota((1, lanes_all), 1) // count) * per_peer
 
     pl.semaphore_wait(barrier, peers - 1 + mps - 1)
 
@@ -84,8 +91,7 @@
     def cache_copy(o):
         to = lax.rem(me + o, peers)
         return remote(
-            outgoing.at[pl.ds(to * per_peer, per_peer)],
-            arrived.at[pl.ds(me * per_peer, per_peer)],
+            outgoing.at[to], arrived.at[me],
             c_send.at[o], c_recv.at[o], {"streams": to},
         )
 
@@ -99,23 +105,38 @@
 
     def start_small(o, c):
         down_copy(o).start()
+        dest_copy(o).start()
         return c
 
     def start_rest(o, c):
+        q = lax.rem(me + o, peers)
+        rows_q = iota((chunk, lanes_all), 0) + q * chunk
+        sel = jnp.where(rows_q == key, 1.0, 0.0).astype(BF16)
+        outgoing[q] = jnp.dot(
+            sel, cache[...].reshape(lanes_all, width), preferred_element_type=F32
+        ).astype(BF16)
+
+        @pl.when(o < peers)
+        def _():
+            cache_copy(o).start()
+
+        return c
+
+    lax.fori_loop(1, peers, start_small, 0)
+    for o in range(1, mps):
+        frame_copy(o).start()
+    lax.fori_loop(1, peers + 1, start_rest, 0)
+
+    def start_up(o, c):
         up_copy(o).start()
-        dest_copy(o).start()
-        cache_copy(o).start()
-        return c
-
-    lax.fori_loop(1, peers, start_small, 0)
-    for o in range(1, mps):
-        frame_copy(o).start()
-    lax.fori_loop(1, peers, start_rest, 0)
+        return c
+
+    lax.fori_loop(1, peers, start_up, 0)
 
     downg[me] = down[...]
     upg[me] = up[...]
     destall[me] = dest[...]
-    arrived[pl.ds(me * per_peer, per_peer)] = outgoing[pl.ds(me * per_peer, per_peer)]
+    arrived[me] = outgoing[me]
 
     w_copy.wait()
     acc[...] = jnp.dot(
@@ -149,7 +170,7 @@
         return c
 
     lax.fori_loop(1, peers, wait_small, 0)
-    to_me = destall[:, 0, :] == me
+    to_me = (destall[:, 0, :] == me) & (iota((peers, 128), 1) < count)
     hits = jnp.where(to_me, 1.0, 0.0)
     tri = jnp.where(iota((128, 128), 0) < iota((128, 128), 1), 1.0, 0.0)
     earlier = jnp.dot(hits.astype(BF16), tri.astype(BF16), preferred_element_type=F32)
@@ -160,8 +181,13 @@
         eye.astype(BF16), jnp.broadcast_to(bucket, (128, 128)).astype(BF16),
         (((1,), (1,)), ((), ())), preferred_element_type=F32,
     )
-    length = outgoing.shape[1]
-    source = column[:count, :].astype(jnp.int32) * length
+    found = column[:count, :].astype(jnp.int32)
+    source = (found // per_peer) * chunk + found % per_peer
+    blocks = peers * chunk
+    wanted = jnp.concatenate([source] * (blocks // 128), axis=1)
+    wanted = iota((count, blocks), 1) - wanted
+    for t in range(hist):
+        select[t] = jnp.where(wanted == t * per_peer, 1.0, 0.0).astype(BF16)
 
     for o in range(1, mps):
         low_copy(o).wait()
@@ -193,14 +219,10 @@
         return c
 
     lax.fori_loop(1, peers, wait_cache, 0)
-    blocks = peers * per_peer * length
-    flat = arrived[...].reshape(blocks, width)
-    wanted = jnp.concatenate([source] * (blocks // 128), axis=1)
-    wanted = wanted - iota((count, blocks), 1)
-    select = jnp.concatenate(
-        [jnp.where(wanted == -t, 1.0, 0.0).astype(BF16) for t in range(hist)], axis=0
-    )
-    moved = jnp.dot(select, flat, preferred_element_type=F32)
+    moved = jnp.dot(
+        select[...].reshape(lanes_all, blocks), arrived[...].reshape(blocks, width),
+        preferred_element_type=F32,
+    )
     seq[pl.ds(0, hist)] = moved.reshape(hist, count, width)
 
     limit = jnp.zeros((count, 128), jnp.int32)
@@ -217,7 +239,7 @@
             for k in range(hist + 1):
                 window = seq[pl.ds(k, fr), pl.ds(sb * seg, seg), lanes]
                 total = total + window * taps[pl.ds(k, 1), lanes][None]
-            normed = total * scale[:, lanes][None] + offset[:, lanes][None]
+            normed = total * scale[lanes].reshape(1, 1, 128) + offset[lanes].reshape(1, 1, 128)
             active = normed * jax.nn.sigmoid(normed)
             enc[:, pl.ds(sb * seg, seg), lanes] = jnp.where(keep, active, 0.0)
             return c
@@ -242,28 +264,22 @@
     length = -(-hist // 16) * 16
     per_peer = max(1, count // peers)
     rank_dim = tenant_down_weight.shape[2]
-    order = jnp.arange(count, dtype=jnp.int32)
-    earlier = (destination[:, None] == destination[None, :]) & (order[None, :] < order[:, None])
-    bucket = destination * per_peer + jnp.sum(earlier.astype(jnp.int32), axis=1)
-    target = jnp.arange(peers * per_peer, dtype=jnp.int32)
-    pick = jnp.sum(jnp.where(bucket[None, :] == target[:, None], order[None, :], 0), axis=1)
-    dest = jnp.broadcast_to(
-        jnp.pad(destination, (0, 128 - count), constant_values=-1)[None, :], (8, 128)
-    )
     smem = pl.BlockSpec(memory_space=pltpu.SMEM)
     vmem = pl.BlockSpec(memory_space=pltpu.VMEM)
-    dims = (peers, mps, count, fr, hist, width, per_peer, rank_dim)
+    dims = (peers, mps, count, fr, hist, length, width, per_peer, rank_dim)
     dma = pltpu.SemaphoreType.DMA
     return pl.pallas_call(
         functools.partial(kernel, dims),
         out_shape=jax.ShapeDtypeStruct((rows, width), BF16),
-        in_specs=[smem] * 4 + [vmem] * 3 + [pl.BlockSpec(memory_space=pl.ANY)] + [vmem] * 5,
+        in_specs=[smem] * 4 + [vmem] * 2 + [pl.BlockSpec(memory_space=pl.ANY)] + [vmem] * 5,
         out_specs=vmem,
         scratch_shapes=[
             pltpu.VMEM((mps, rows, width), BF16),
-            pltpu.VMEM((peers * per_peer, length, width), BF16),
-            pltpu.VMEM((peers * per_peer, length, width), BF16),
+            pltpu.VMEM((peers, length * per_peer, width), BF16),
+            pltpu.VMEM((peers, length * per_peer, width), BF16),
+            pltpu.VMEM((8, 128), jnp.int32),
             pltpu.VMEM((peers, 8, 128), jnp.int32),
+            pltpu.VMEM((hist, count, peers * length * per_peer), BF16),
             pltpu.VMEM((peers, rank_dim, width), BF16),
             pltpu.VMEM((peers, rank_dim, 2 * width), BF16),
             pltpu.VMEM((mps, rank_dim, rows), F32),
@@ -283,11 +299,11 @@
             collective_id=0, has_side_effects=True, vmem_limit_bytes=56 * 1024 * 1024
         ),
     )(
-        pick, tenant, valid, tenant_panel_slot,
-        frames, convolution_cache, dest,
+        destination, tenant, valid, tenant_panel_slot,
+        frames, convolution_cache.transpose(1, 0, 2),
         input_weight.reshape(mps * width, 2 * width),
         tenant_down_weight[0].T, tenant_up_weight.reshape(rank_dim, 2 * width),
-        depthwise_taps, batchnorm_scale.reshape(1, width), batchnorm_offset.reshape(1, width),
+        depthwise_taps, batchnorm_scale, batchnorm_offset,
     )
 
 

time: 51 us -> 46.1 us (0.904)
  the two profiles are of different devices: /device:TPU:28 before, /device:TPU:0 now
where the time goes in v2:
time: 46.1 us; the launch traced here: 45.9 us
  Pallas kernels  39.2 us (85%)
  local copies, waits for them, and re-layouts  6.6 us (14%)
    pallas_call x1, Pallas kernels, local(): pl.pallas_call(functools.partial(kernel, dims), out_shape=jax.ShapeDtypeS...  39.2 us
    unnamed x3, local copies, waits for them, and re-layouts  6.6 us

profile of v2, /device:TPU:0, one launch (start us, length us, event | category | flops | bytes accessed | tf_op | source)
XLA Modules:
  0.0 45.9 jit_solution(8664059844409030200)
XLA Ops:
  0.0 1.3 %copy.14 = bf16[2,8,2,384]{3,1,2,0:T(8,128)(2,1)} copy(bf16[2,8,2,384]{3,2,1,0:T(2,128)(2,1)} %bitcast.13) | data formatting | bytes 49152
  1.4 3.5 %copy.13 = bf16[192,8,2,384]{3,1,2,0:T(8,128)(2,1)} copy(bf16[192,8,2,384]{3,2,1,0:T(2,128)(2,1)} %bitcast.10) | data formatting | bytes 4718592
  4.9 39.2 %shard_map.118 = bf16[384,384]{1,0:T(8,128)(2,1)} custom-call(s32[32]{0:T(128)} %dest_s.1, s32[32]{0:T(128)} %tenant_s.1, s32[32]{0:T(128)} %valid_s.1, s32[4]{0:T(128)} %panel_s.1, bf16[384,384]{1,0:T(8,128)(2,1)} %frames.1, bf16[31,32,384]{2,1,0:T(8,128)(2,1)} %bitcast.11, bf16[1536,768]{1,0:T(8,128)(2,1)} %bitcast.9, bf16[16,384]{1,0:T(8,128)(2,1)} %bitcast.14, ...), custom_call_target="tpu_custom_call" | custom-call | tf_op jit(solution)/shard_map/pallas_call | solution.py:271
  44.2 1.7 %copy.16 = bf16[384,384]{1,0:T(8,128)(2,1)} copy(bf16[384,384]{1,0:T(8,128)(2,1)} %shard_map.118) | data formatting | bytes 589824

commit v3 on v2

--- a/solution.py
+++ b/solution.py
@@ -20,9 +20,9 @@
 def kernel(
     dims,
     dest_s, tenant_s, valid_s, panel_s,
-    frames, cache, weight_hbm, down, up, taps, scale, offset,
+    frames, cache, weight_hbm, down, up_raw, taps, scale, offset,
     out,
-    gathered, outgoing, arrived, dest, destall, select, downg, upg, lows, weight, acc, seq, enc,
+    gathered, outgoing, arrived, dest, destall, select, downg, upg, lows, up, cache32, raw, weight, acc, seq, enc,
     w_sem, f_send, f_recv, c_send, c_recv, d_send, d_recv, a_send, a_recv, u_send, u_recv,
     l_send, l_recv,
 ):
@@ -31,7 +31,7 @@
     me = lax.axis_index("streams")
     my = lax.axis_index("mp")
 
-    w_copy = pltpu.make_async_copy(weight_hbm, weight, w_sem)
+    w_copy = pltpu.make_async_copy(weight_hbm, raw, w_sem)
     w_copy.start()
 
     barrier = pltpu.get_barrier_semaphore()
@@ -52,21 +52,20 @@
     perm = jnp.where(c_i == (r_i % count) * fr + r_i // count, 1.0, 0.0).astype(BF16)
     mine = jnp.dot(perm, frames[...], preferred_element_type=F32).astype(BF16)
     gathered[my] = mine
+    halves = up_raw[...].astype(F32)
+    up[:, :width] = halves[:, 0, :].astype(BF16)
+    up[:, width:] = halves[:, 1, :].astype(BF16)
+    for j in range(width // 128):
+        piece = cache[:, :, j * 128:(j + 1) * 128].reshape(hist * count, 128)
+        cache32[j] = piece.astype(F32)
+    blank = jnp.zeros((length - hist, width), F32)
 
     stream = iota((8, 128), 1) % count
     goes = jnp.zeros((8, 128), jnp.int32)
     for s in range(count):
         goes = jnp.where(stream == s, dest_s[s], goes)
     dest[...] = goes
-    place = jnp.zeros((8, 128), jnp.int32)
-    for s in range(count):
-        place = place + jnp.where((goes == dest_s[s]) & (stream > s), 1, 0)
     chunk = length * per_peer
-    key = (goes * chunk + place)[:1]
-    lanes_all = hist * count
-    wide = -(-lanes_all // 128)
-    key = jnp.concatenate([key] * wide, axis=1)[:, :lanes_all]
-    key = key + (iota((1, lanes_all), 1) // count) * per_peer
 
     pl.semaphore_wait(barrier, peers - 1 + mps - 1)
 
@@ -110,11 +109,23 @@
 
     def start_rest(o, c):
         q = lax.rem(me + o, peers)
-        rows_q = iota((chunk, lanes_all), 0) + q * chunk
-        sel = jnp.where(rows_q == key, 1.0, 0.0).astype(BF16)
-        outgoing[q] = jnp.dot(
-            sel, cache[...].reshape(lanes_all, width), preferred_element_type=F32
-        ).astype(BF16)
+        picks = [jnp.int32(0)] * per_peer
+        for s in reversed(range(count)):
+            fits = dest_s[s] == q
+            picks = [
+                jnp.where(fits, new, old) for new, old in zip([jnp.int32(s)] + picks[:-1], picks)
+            ]
+        for r, p in enumerate(picks):
+            one = jnp.concatenate(
+                [
+                    cache32.at[j][pl.ds(p, hist, stride=count), :]
+                    for j in range(width // 128)
+                ],
+                axis=1,
+            )
+            outgoing[q, r * length:(r + 1) * length, :] = jnp.concatenate(
+                [one, blank], axis=0
+            ).astype(BF16)
 
         @pl.when(o < peers)
         def _():
@@ -139,6 +150,15 @@
     arrived[me] = outgoing[me]
 
     w_copy.wait()
+
+    def split(i, c):
+        at = pl.ds(pl.multiple_of(i * 64, 64), 64)
+        both = raw[at].astype(F32)
+        weight[at, :width] = both[:, 0, :].astype(BF16)
+        weight[at, width:] = both[:, 1, :].astype(BF16)
+        return c
+
+    lax.fori_loop(0, mps * width // 64, split, 0)
     acc[...] = jnp.dot(
         mine, weight[pl.ds(pl.multiple_of(my * width, width), width), :],
         preferred_element_type=F32,
@@ -182,12 +202,13 @@
         (((1,), (1,)), ((), ())), preferred_element_type=F32,
     )
     found = column[:count, :].astype(jnp.int32)
-    source = (found // per_peer) * chunk + found % per_peer
+    source = found * length
     blocks = peers * chunk
+    lanes_all = hist * count
     wanted = jnp.concatenate([source] * (blocks // 128), axis=1)
     wanted = iota((count, blocks), 1) - wanted
     for t in range(hist):
-        select[t] = jnp.where(wanted == t * per_peer, 1.0, 0.0).astype(BF16)
+        select[t] = jnp.where(wanted == t, 1.0, 0.0).astype(BF16)
 
     for o in range(1, mps):
         low_copy(o).wait()
@@ -283,6 +304,9 @@
             pltpu.VMEM((peers, rank_dim, width), BF16),
             pltpu.VMEM((peers, rank_dim, 2 * width), BF16),
             pltpu.VMEM((mps, rank_dim, rows), F32),
+            pltpu.VMEM((rank_dim, 2 * width), BF16),
+            pltpu.VMEM((width // 128, hist * count, 128), F32),
+            pltpu.VMEM((mps * width, 2, width), BF16),
             pltpu.VMEM((mps * width, 2 * width), BF16),
             pltpu.VMEM((rows, 2 * width), F32),
             pltpu.VMEM((hist + fr, count, width), F32),
@@ -301,8 +325,8 @@
     )(
         destination, tenant, valid, tenant_panel_slot,
         frames, convolution_cache.transpose(1, 0, 2),
-        input_weight.reshape(mps * width, 2 * width),
-        tenant_down_weight[0].T, tenant_up_weight.reshape(rank_dim, 2 * width),
+        input_weight,
+        tenant_down_weight[0].T, tenant_up_weight[0],
         depthwise_taps, batchnorm_scale, batchnorm_offset,
     )
 

time: 46.1 us -> 41.2 us (0.89)
  local copies, waits for them, and re-layouts: 6.6 us -> 1.71 us
    unnamed x3 -> x1, local copies, waits for them, and re-layouts: 6.6 us -> 1.71 us
where the time goes in v3:
time: 41.2 us; the launch traced here: 41.1 us
  Pallas kernels  39.4 us (96%)
  local copies, waits for them, and re-layouts  1.71 us (4%)
    pallas_call x1, Pallas kernels, local(): pl.pallas_call(functools.partial(kernel, dims), out_shape=jax.ShapeDtypeS...  39.4 us
    unnamed x1, local copies, waits for them, and re-layouts  1.71 us

profile of v3, /device:TPU:0, one launch (start us, length us, event | category | flops | bytes accessed | tf_op | source)
XLA Modules:
  0.0 41.1 jit_solution(218619384817050009)
XLA Ops:
  0.0 39.4 %shard_map.118 = bf16[384,384]{1,0:T(8,128)(2,1)} custom-call(s32[32]{0:T(128)} %dest_s.1, s32[32]{0:T(128)} %tenant_s.1, s32[32]{0:T(128)} %valid_s.1, s32[4]{0:T(128)} %panel_s.1, bf16[384,384]{1,0:T(8,128)(2,1)} %frames.1, bf16[31,32,384]{2,1,0:T(8,128)(2,1)} %bitcast.5, bf16[1536,2,384]{2,1,0:T(2,128)(2,1)} %weight_hbm.1, bf16[16,384]{1,0:T(8,128)(2,1)} %bitcast.7, ...), custom_call_target="tpu_custom_call" | custom-call | tf_op jit(solution)/shard_map/pallas_call | solution.py:292
  39.4 1.7 %copy.14 = bf16[384,384]{1,0:T(8,128)(2,1)} copy(bf16[384,384]{1,0:T(8,128)(2,1)} %shard_map.118) | data formatting | bytes 589824

commit v4 on v3

--- a/solution.py
+++ b/solution.py
@@ -23,7 +23,7 @@
     frames, cache, weight_hbm, down, up_raw, taps, scale, offset,
     out,
     gathered, outgoing, arrived, dest, destall, select, downg, upg, lows, up, cache32, raw, weight, acc, seq, enc,
-    w_sem, f_send, f_recv, c_send, c_recv, d_send, d_recv, a_send, a_recv, u_send, u_recv,
+    w_sem, f_send, f_recv, c_send, c_recv, g_send, g_recv,
     l_send, l_recv,
 ):
     peers, mps, count, fr, hist, length, width, per_peer, rank_dim = dims
@@ -75,17 +75,27 @@
             device_id=where, device_id_type=MESH,
         )
 
-    def down_copy(o):
-        to = {"streams": lax.rem(me + o, peers)}
-        return remote(down, downg.at[me], a_send.at[o], a_recv.at[o], to)
-
-    def up_copy(o):
-        to = {"streams": lax.rem(me + o, peers)}
-        return remote(up, upg.at[me], u_send.at[o], u_recv.at[o], to)
-
-    def dest_copy(o):
-        to = {"streams": lax.rem(me + o, peers)}
-        return remote(dest, destall.at[me], d_send.at[o], d_recv.at[o], to)
+    half = peers // 2
+    side, place = lax.rem(me, 2), me // 2
+    pair = {"streams": me + 1 - 2 * side}
+    small = ((down, downg), (dest, destall), (up, upg))
+
+    def small_copy(i, o):
+        src, dst = small[i]
+        to = {"streams": 2 * lax.rem(place + o, half) + side}
+        return remote(src, dst.at[side, place], g_send.at[i, o], g_recv.at[i, o], to)
+
+    def pair_copy(i):
+        dst = small[i][1]
+        return remote(dst.at[side], dst.at[side], g_send.at[i, 0], g_recv.at[i, 0], pair)
+
+    def relay(i):
+        def arrive(o, c):
+            small_copy(i, o).wait()
+            return c
+
+        lax.fori_loop(1, half, arrive, 0)
+        pair_copy(i).start()
 
     def cache_copy(o):
         to = lax.rem(me + o, peers)
@@ -102,10 +112,16 @@
         to = {"mp": lax.rem(my + o, mps)}
         return remote(lows.at[my], lows.at[my], l_send.at[o], l_recv.at[o], to)
 
+    downg[side, place] = down[...]
+    destall[side, place] = dest[...]
+    upg[side, place] = up[...]
+
     def start_small(o, c):
-        down_copy(o).start()
-        dest_copy(o).start()
-        return c
+        for i in range(3):
+            small_copy(i, o).start()
+        return c
+
+    lax.fori_loop(1, half, start_small, 0)
 
     def start_rest(o, c):
         q = lax.rem(me + o, peers)
@@ -133,21 +149,13 @@
 
         return c
 
-    lax.fori_loop(1, peers, start_small, 0)
     for o in range(1, mps):
         frame_copy(o).start()
     lax.fori_loop(1, peers + 1, start_rest, 0)
 
-    def start_up(o, c):
-        up_copy(o).start()
-        return c
-
-    lax.fori_loop(1, peers, start_up, 0)
-
-    downg[me] = down[...]
-    upg[me] = up[...]
-    destall[me] = dest[...]
     arrived[me] = outgoing[me]
+    for i in range(3):
+        relay(i)
 
     w_copy.wait()
 
@@ -169,32 +177,25 @@
     for s in range(count):
         slot = jnp.where(lane == s, panel_s[tenant_s[s]], slot)
 
-    def wait_down(o, c):
-        down_copy(o).wait()
-        return c
-
-    lax.fori_loop(1, peers, wait_down, 0)
+    for i in range(3):
+        pair_copy(i).wait()
     panels = downg[...].reshape(peers * rank_dim, width)
     projected = lax.dot_general(
         panels, mine, (((1,), (1,)), ((), ())), preferred_element_type=F32
     )
-    hit = iota((peers * rank_dim, rows), 0) // rank_dim == slot
+    at = iota((peers * rank_dim, rows), 0) // rank_dim
+    hit = at == (slot % 2) * half + slot // 2
     part = jnp.where(hit, projected, 0.0).reshape(peers, rank_dim, rows).sum(axis=0)
     lows[my] = part
     for o in range(1, mps):
         low_copy(o).start()
 
-    def wait_small(o, c):
-        dest_copy(o).wait()
-        up_copy(o).wait()
-        return c
-
-    lax.fori_loop(1, peers, wait_small, 0)
-    to_me = (destall[:, 0, :] == me) & (iota((peers, 128), 1) < count)
+    to_me = (destall[...].reshape(peers, 8, 128)[:, 0, :] == me) & (iota((peers, 128), 1) < count)
     hits = jnp.where(to_me, 1.0, 0.0)
     tri = jnp.where(iota((128, 128), 0) < iota((128, 128), 1), 1.0, 0.0)
     earlier = jnp.dot(hits.astype(BF16), tri.astype(BF16), preferred_element_type=F32)
-    owner = iota((peers, 128), 0).astype(F32)
+    at = iota((peers, 128), 0)
+    owner = (2 * (at % half) + at // half).astype(F32)
     bucket = jnp.sum(hits * (owner * per_peer + earlier), axis=0, keepdims=True)
     eye = jnp.where(iota((128, 128), 0) == iota((128, 128), 1), 1.0, 0.0)
     column = lax.dot_general(
@@ -299,10 +300,10 @@
             pltpu.VMEM((peers, length * per_peer, width), BF16),
             pltpu.VMEM((peers, length * per_peer, width), BF16),
             pltpu.VMEM((8, 128), jnp.int32),
-            pltpu.VMEM((peers, 8, 128), jnp.int32),
+            pltpu.VMEM((2, peers // 2, 8, 128), jnp.int32),
             pltpu.VMEM((hist, count, peers * length * per_peer), BF16),
-            pltpu.VMEM((peers, rank_dim, width), BF16),
-            pltpu.VMEM((peers, rank_dim, 2 * width), BF16),
+            pltpu.VMEM((2, peers // 2, rank_dim, width), BF16),
+            pltpu.VMEM((2, peers // 2, rank_dim, 2 * width), BF16),
             pltpu.VMEM((mps, rank_dim, rows), F32),
             pltpu.VMEM((rank_dim, 2 * width), BF16),
             pltpu.VMEM((width // 128, hist * count, 128), F32),
@@ -314,9 +315,7 @@
             dma,
             dma((mps,)), dma((mps,)),
             dma((peers,)), dma((peers,)),
-            dma((peers,)), dma((peers,)),
-            dma((peers,)), dma((peers,)),
-            dma((peers,)), dma((peers,)),
+            dma((3, peers // 2)), dma((3, peers // 2)),
             dma((mps,)), dma((mps,)),
         ],
         compiler_params=pltpu.CompilerParams(

time: 41.2 us -> 37.6 us (0.913)
  Pallas kernels: 39.4 us -> 35.7 us
    pallas_call x1, Pallas kernels: 39.4 us -> 35.7 us  [local(): pl.pallas_call(functools.partial(kernel, dims), out_shape=jax.ShapeDtypeS...]
where the time goes in v4:
time: 37.6 us; the launch traced here: 37.4 us
  Pallas kernels  35.7 us (95%)
  local copies, waits for them, and re-layouts  1.71 us (5%)
    pallas_call x1, Pallas kernels, local(): pl.pallas_call(functools.partial(kernel, dims), out_shape=jax.ShapeDtypeS...  35.7 us
    unnamed x1, local copies, waits for them, and re-layouts  1.71 us

profile of v4, /device:TPU:0, one launch (start us, length us, event | category | flops | bytes accessed | tf_op | source)
XLA Modules:
  0.0 37.4 jit_solution(17248300897022075533)
XLA Ops:
  0.0 35.7 %shard_map.118 = bf16[384,384]{1,0:T(8,128)(2,1)} custom-call(s32[32]{0:T(128)} %dest_s.1, s32[32]{0:T(128)} %tenant_s.1, s32[32]{0:T(128)} %valid_s.1, s32[4]{0:T(128)} %panel_s.1, bf16[384,384]{1,0:T(8,128)(2,1)} %frames.1, bf16[31,32,384]{2,1,0:T(8,128)(2,1)} %bitcast.5, bf16[1536,2,384]{2,1,0:T(2,128)(2,1)} %weight_hbm.1, bf16[16,384]{1,0:T(8,128)(2,1)} %bitcast.7, ...), custom_call_target="tpu_custom_call" | custom-call | tf_op jit(solution)/shard_map/pallas_call | solution.py:293
  35.7 1.7 %copy.14 = bf16[384,384]{1,0:T(8,128)(2,1)} copy(bf16[384,384]{1,0:T(8,128)(2,1)} %shard_map.118) | data formatting | bytes 589824

commit v5 on v4

--- a/solution.py
+++ b/solution.py
@@ -154,8 +154,6 @@
     lax.fori_loop(1, peers + 1, start_rest, 0)
 
     arrived[me] = outgoing[me]
-    for i in range(3):
-        relay(i)
 
     w_copy.wait()
 
@@ -167,6 +165,8 @@
         return c
 
     lax.fori_loop(0, mps * width // 64, split, 0)
+    for i in range(3):
+        relay(i)
     acc[...] = jnp.dot(
         mine, weight[pl.ds(pl.multiple_of(my * width, width), width), :],
         preferred_element_type=F32,
@@ -212,6 +212,13 @@
         select[t] = jnp.where(wanted == t, 1.0, 0.0).astype(BF16)
 
     for o in range(1, mps):
+        frame_copy(o).wait()
+        j = lax.rem(my + mps - o, mps)
+        acc[...] += jnp.dot(
+            gathered[j], weight[pl.ds(pl.multiple_of(j * width, width), width), :],
+            preferred_element_type=F32,
+        )
+    for o in range(1, mps):
         low_copy(o).wait()
     low = lows[0]
     for j in range(1, mps):
@@ -225,13 +232,6 @@
         preferred_element_type=F32,
     )
 
-    for o in range(1, mps):
-        frame_copy(o).wait()
-        j = lax.rem(my + mps - o, mps)
-        acc[...] += jnp.dot(
-            gathered[j], weight[pl.ds(pl.multiple_of(j * width, width), width), :],
-            preferred_element_type=F32,
-        )
     pre = acc[...]
     gated = (pre[:, :width] * jax.nn.sigmoid(pre[:, width:])).astype(BF16)
     seq[pl.ds(hist, fr)] = gated.astype(F32).reshape(fr, count, width)

time: 37.6 us -> 34.2 us (0.910)
  Pallas kernels: 35.7 us -> 32.4 us
    pallas_call x1, Pallas kernels: 35.7 us -> 32.4 us  [local(): pl.pallas_call(functools.partial(kernel, dims), out_shape=jax.ShapeDtypeS...]
where the time goes in v5:
time: 34.2 us; the launch traced here: 34.1 us
  Pallas kernels  32.4 us (95%)
  local copies, waits for them, and re-layouts  1.71 us (5%)
    pallas_call x1, Pallas kernels, local(): pl.pallas_call(functools.partial(kernel, dims), out_shape=jax.ShapeDtypeS...  32.4 us
    unnamed x1, local copies, waits for them, and re-layouts  1.71 us

profile of v5, /device:TPU:0, one launch (start us, length us, event | category | flops | bytes accessed | tf_op | source)
XLA Modules:
  0.0 34.1 jit_solution(7063129189315641689)
XLA Ops:
  0.0 32.4 %shard_map.118 = bf16[384,384]{1,0:T(8,128)(2,1)} custom-call(s32[32]{0:T(128)} %dest_s.1, s32[32]{0:T(128)} %tenant_s.1, s32[32]{0:T(128)} %valid_s.1, s32[4]{0:T(128)} %panel_s.1, bf16[384,384]{1,0:T(8,128)(2,1)} %frames.1, bf16[31,32,384]{2,1,0:T(8,128)(2,1)} %bitcast.5, bf16[1536,2,384]{2,1,0:T(2,128)(2,1)} %weight_hbm.1, bf16[16,384]{1,0:T(8,128)(2,1)} %bitcast.7, ...), custom_call_target="tpu_custom_call" | custom-call | tf_op jit(solution)/shard_map/pallas_call | solution.py:293
  32.4 1.7 %copy.14 = bf16[384,384]{1,0:T(8,128)(2,1)} copy(bf16[384,384]{1,0:T(8,128)(2,1)} %shard_map.118) | data formatting | bytes 589824
